TPU v7x, 256 devices: a whole 4x4x8 slice. The times are simulated.
256 devices in a mesh: blk: 32 (over z_hi, x, core), grp: 8 (over z_lo, y).
Axes of the slice: x: 4, y: 4, z: 8 (z_hi: 4, z_lo: 2; z = z_hi * 2 + z_lo), core: 2. Of those that a mesh axis runs over, the one named last changes fastest.
Arguments:
- inv_tiles: bfloat16 [64, 64, 512, 512], P(None, 'grp', 'blk'), may hold values from -6 to 6
- factor: bfloat16 [8, 16, 512, 512], P('grp', None, 'blk'), may hold values from -0.0625 to 0.0625
- diag_inv_factor: float32 [8, 512, 512], P('grp', 'blk'), may hold values from -6 to 6
- structure: int32 [8, 16], replicated, may hold values from 0 to 63, as said below
Outputs:
- offdiag_inv: bfloat16 [8, 16, 512, 512], P('grp', None, 'blk')
- diag_inv: float32 [8, 512, 512], P('grp', 'blk')
Inputs may be any that keep to these rules, and one draw needn't show every extreme that they name: `structure`: each row lists 16 distinct ancestor blocks in ascending order, exactly 2 in each run of 8 blocks that starts at a multiple of 8; block 63 is listed in every row.
All inputs are finite; a program needn't handle non-finite values.
Results may differ from a plain program's by a relative error of at most 0.018.
Values may be sent and summed in bfloat16 or wider, within the bound.
A program may use at most 128 MiB of HBM per device.

v0:
```python
import jax
import jax.numpy as jnp
from jax import lax
from jax.sharding import PartitionSpec as P


def split_up(shard, dim, count):
    dims = shard.shape
    tiles = shard.reshape(*dims[:dim], count, dims[dim] // count, *dims[dim + 1 :])
    return jnp.moveaxis(tiles, dim, 0)


def sum_at_owner(shard, axis, dim):
    count = lax.axis_size(axis)
    tiles = lax.all_to_all(split_up(shard, dim, count), axis, 0, 0, tiled=True)
    return jnp.sum(tiles.astype(jnp.float32), axis=0)


def on_device(inv_tiles, factor, diag_inv_factor, structure):
    grp_count = lax.axis_size("grp")
    grp_index = lax.axis_index("grp")
    col_local = inv_tiles.shape[1]
    width = inv_tiles.shape[3]
    own_count = factor.shape[0]
    listed_count = factor.shape[1]
    slab_rows = factor.shape[2]
    per_group = listed_count // grp_count
    node_total = own_count * grp_count
    grouped = factor.reshape(own_count, grp_count, per_group, slab_rows, width)
    received = lax.all_to_all(grouped, "grp", split_axis=1, concat_axis=0, tiled=True)
    received = received.reshape(node_total, per_group, slab_rows, width)
    readers = lax.all_gather(received, "blk", axis=2, tiled=True)
    col_base = grp_index * col_local
    local_cols = lax.dynamic_slice_in_dim(structure, grp_index * per_group, per_group, 1) - col_base
    selected = inv_tiles[structure[:, :, None], local_cols[:, None, :]]
    summed = sum_at_owner(
        jnp.einsum(
            "crjxy,cjyz->crxz", selected, readers, preferred_element_type=jnp.float32
        ).astype(jnp.bfloat16),
        "grp",
        0,
    )
    offdiag = (-summed).astype(jnp.bfloat16)
    correction = sum_at_owner(
        jnp.einsum("krxy,krxz->ykz", factor, offdiag, preferred_element_type=jnp.float32).astype(
            jnp.bfloat16
        ),
        "blk",
        0,
    )
    diag_inv = diag_inv_factor - jnp.transpose(correction, (1, 0, 2))
    return (offdiag, diag_inv)


def solution(mesh):
    return jax.shard_map(
        on_device,
        mesh=mesh,
        in_specs=(
            P(None, "grp", "blk", None),
            P("grp", None, "blk", None),
            P("grp", "blk", None),
            P(),
        ),
        out_specs=(P("grp", None, "blk", None), P("grp", "blk", None)),
        check_vma=False,
    )
```

profile of v0, /device:TPU:1, one launch (start us, length us, event | category | flops | bytes accessed | tf_op | source)
XLA Modules:
  0.0 173.3 jit_solution(4277369298304297157)
XLA Ops:
  7.2 0.0 all-gather.3.cloned.1.call-start
  7.2 12.6 %all_to_all.19 = bf16[1,8,2,16,512]{4,3,2,0,1:T(8,128)(2,1)} all-to-all(bf16[1,8,2,16,512]{4,3,2,0,1:T(8,128)(2,1)} %bitcast.46), channel_id=1, replica_groups=mesh['blk'=32,'grp'=8] {'grp'}, dimensions={1} | all-to-all | bytes 524288 | tf_op jit(solution)/shard_map/all_to_all | solution.py:30
  19.8 0.0 all-gather.3.cloned.1.call-update
  19.8 0.8 fusion.13
  20.6 0.7 fusion.11
  21.3 0.1 broadcast_or_fusion
  21.4 0.1 reshape.63
  21.5 6.5 %gather_fusion = bf16[256,16,512]{2,1,0:T(8,128)(2,1)} fusion(bf16[64,8,16,512]{3,2,1,0:T(8,128)(2,1)} %param.4, s32[256]{0:T(256)S(1)} %reshape.63), kind=kCustom, calls=%fused_computation | custom fusion | bytes 8390656 | tf_op jit(solution)/shard_map/gather | solution.py:35
  28.0 69.7 %all-gather.3.cloned.1.call-done = bf16[1,8,2,512,512]{4,3,2,1,0:T(8,128)(2,1)} async-done(((bf16[1,8,2,16,512]{4,3,2,1,0:T(8,128)(2,1)}), bf16[1,8,2,512,512]{4,3,2,1,0:T(8,128)(2,1)}) %all-gather.3.cloned.1.call-update) | async-done | bytes 8388624 | tf_op jit(solution)/shard_map/all_gather | solution.py:32
  97.7 7.0 %fusion.4 = bf16[8,1,16,16,512]{4,3,2,1,0:T(8,128)(2,1)S(1)} fusion(bf16[8,16,2,16,512]{4,3,2,1,0:T(8,128)(2,1)} %bitcast.45, bf16[1,8,2,512,512]{4,3,2,1,0:T(8,128)(2,1)} %all-gather.3.cloned.1.call-done), kind=kOutput, calls=%fused_computation.5 | convolution fusion | flops 2148532224 | bytes 14680064 | tf_op jit(solution)/shard_map/crjxy,cjyz->crxz/dot_general | solution.py:37
  104.7 0.0 copy-start
  104.7 33.1 %all_to_all.20 = bf16[8,1,16,16,512]{4,3,2,1,0:T(8,128)(2,1)S(1)} all-to-all(bf16[8,1,16,16,512]{4,3,2,1,0:T(8,128)(2,1)S(1)} %fusion.4), channel_id=1, replica_groups=mesh['blk'=32,'grp'=8] {'grp'}, dimensions={0} | all-to-all | bytes 4194304 | tf_op jit(solution)/shard_map/all_to_all | solution.py:15
  137.8 0.0 copy-start.1
  137.8 0.4 convert_reduce_fusion
  138.1 0.0 copy-done
  138.1 1.1 fusion.7
  139.3 8.1 %all-to-all-start.2 = ((bf16[32,16,1,512]{3,1,2,0:T(8,128)(2,1)}), bf16[32,16,1,512]{3,1,2,0:T(8,128)(2,1)S(1)}, u32[]{:S(2)}, u32[]{:S(2)}) async-start(bf16[32,16,1,512]{3,1,2,0:T(8,128)(2,1)} %bitcast.16), calls=%async_computation.2 | async-start | bytes 1048576 | tf_op jit(solution)/shard_map/all_to_all | solution.py:15
  147.4 0.7 fusion.9
  148.1 17.6 %all-to-all-done.2 = bf16[32,16,1,512]{3,1,2,0:T(8,128)(2,1)S(1)} async-done(((bf16[32,16,1,512]{3,1,2,0:T(8,128)(2,1)}), bf16[32,16,1,512]{3,1,2,0:T(8,128)(2,1)S(1)}, u32[]{:S(2)}, u32[]{:S(2)}) %all-to-all-start.2) | async-done | bytes 524320 | tf_op jit(solution)/shard_map/all_to_all | solution.py:15
  165.7 0.1 convert_reduce_fusion.1
  165.8 0.0 copy-done.1
  165.8 0.6 bitcast_subtract_fusion
Async XLA Ops:
  7.2 90.5 %all-gather.3.cloned.1.call-start = ((), (), s32[]{:S(2)}) async-start(), calls=%async_computation.3 | async-start | bytes 8650752 | tf_op jit(solution)/shard_map/all_gather | solution.py:32
  104.7 33.4 %copy-start = (bf16[1,16,16,512]{3,2,1,0:T(8,128)(2,1)S(1)}, bf16[1,16,16,512]{3,2,1,0:T(8,128)(2,1)}, u32[]{:S(2)}) copy-start(bf16[1,16,16,512]{3,2,1,0:T(8,128)(2,1)} %param.5) | copy-start | bytes 786436
  137.8 28.1 %copy-start.1 = (f32[1,16,512]{2,1,0:T(8,128)S(1)}, f32[1,16,512]{2,1,0:T(8,128)}, u32[]{:S(2)}) copy-start(f32[1,16,512]{2,1,0:T(8,128)} %param.6) | copy-start | bytes 98308
  139.3 26.5 %all-to-all-start.2 = ((bf16[32,16,1,512]{3,1,2,0:T(8,128)(2,1)}), bf16[32,16,1,512]{3,1,2,0:T(8,128)(2,1)S(1)}, u32[]{:S(2)}, u32[]{:S(2)}) async-start(bf16[32,16,1,512]{3,1,2,0:T(8,128)(2,1)} %bitcast.16), calls=%async_computation.2 | async-start | bytes 1048576 | tf_op jit(solution)/shard_map/all_to_all | solution.py:15
Sparse Core Ops, SparseCore 0:
  19.9 77.6 all-gather.2
where the time goes:
time: 174 us; the launch traced here: 173 us
  waiting for transfers between devices  87.3 us (50%)
  blocking collectives  45.7 us (26%)
  between operations  14.1 us (8%)
  matrix products  8.13 us (5%)
  starting transfers between devices  8.12 us (5%)
  local copies, waits for them, and re-layouts  6.66 us (4%)
  other arithmetic  3.35 us (2%)
    all_gather x1, waiting for transfers between devices, on_device(): readers = lax.all_gather(received, 'blk', axis=2, tiled=True)  69.7 us
    all_to_all x1, blocking collectives, sum_at_owner(): tiles = lax.all_to_all(split_up(shard, dim, count), axis, 0, 0, tiled=True)  33.1 us
    all_to_all x1, waiting for transfers between devices, sum_at_owner(): tiles = lax.all_to_all(split_up(shard, dim, count), axis, 0, 0, tiled=True)  17.6 us
    all_to_all x1, blocking collectives, on_device(): lax.all_to_all(grouped, 'grp', split_axis=1, concat_axis=0, tiled=True)  12.6 us
    all_to_all x1, starting transfers between devices, sum_at_owner(): tiles = lax.all_to_all(split_up(shard, dim, count), axis, 0, 0, tiled=True)  8.09 us
    dot_general x1, matrix products, on_device(): jnp.einsum('crjxy,cjyz->crxz', selected, readers, preferred_element_type=...  6.99 us
    gather x1, local copies, waits for them, and re-layouts, on_device(): selected = inv_tiles[structure[:, :, None], local_cols[:, None, :]]  6.51 us
  transfers between devices with their start and end apart: 2, of which 2 were waited for; matrix products, arithmetic and copies ran while one was open for 5% of the time, Pallas kernels for 0%

commit v1 on v0

v1 whole, which is shorter than its diff:
```python
import functools

import jax
import jax.numpy as jnp
from jax import lax
from jax.experimental import pallas as pl
from jax.experimental.pallas import tpu as pltpu
from jax.sharding import PartitionSpec as P

MESH = pl.DeviceIdType.MESH
BF16 = jnp.bfloat16
F32 = jnp.float32
NZ, NX, NC, NL, NY = 4, 4, 2, 2, 4
ORDER = [(1, 1), (1, 3), (1, 2), (1, 0), (0, 1), (0, 3), (0, 2), (0, 0)]


def place():
    b = lax.axis_index("blk")
    g = lax.axis_index("grp")
    return b // (NX * NC), (b // NC) % NX, b % NC, g // NY, g % NY


def device(zh, x, c, zl, y):
    return {"blk": (zh * NX + x) * NC + c, "grp": zl * NY + y}


def kernel(
    struct_ref, inv_hbm, fac_hbm, dif_ref, off_ref, diag_ref,
    inv_v, f_v, a_v, b_v, c_snd, c_rcv, c_own, z_snd, z_rcv, o_v, o_rcv,
    g32, g_snd, g_rcv, h_snd, h_rcv,
    ld_sem, f_sem, s1_s, s1_r, zs_s, zs_r, x_s, x_r, w_s, w_r, a_s, a_r,
    fx_s, fx_r, c_s, c_r, q_s, q_r, o_s, o_r, g_s, g_r, h_s, h_r,
):
    zh, x, c, zl, y = place()
    sib = 1 - c
    grp = zl * NY + y
    steps = len(ORDER)
    xr, xl = (x + 1) % NX, (x + NX - 1) % NX

    def remote(src, dst, ssem, rsem, dev):
        return pltpu.make_async_remote_copy(
            src_ref=src, dst_ref=dst, send_sem=ssem, recv_sem=rsem,
            device_id=dev, device_id_type=MESH)

    loads = []
    for n in range(8):
        part = pl.ds(8 * n, 8)
        loads.append(pltpu.make_async_copy(inv_hbm.at[part], inv_v.at[part], ld_sem.at[n]))
    load_f = pltpu.make_async_copy(fac_hbm.at[0], f_v.at[c], f_sem)
    for cp in loads:
        cp.start()
    load_f.start()

    partners = []
    for dl in range(NL):
        for dy in range(NY):
            for dc in range(NC):
                if dl or dy or dc:
                    partners.append(device(zh, x, (c + dc) % NC, (zl + dl) % NL, (y + dy) % NY))
    for dz in range(1, NZ):
        for dc in range(NC):
            partners.append(device((zh + dz) % NZ, x, (c + dc) % NC, zl, y))
    for dx in range(1, NX):
        partners.append(device(zh, (x + dx) % NX, c, zl, y))
    bar = pltpu.get_barrier_semaphore()
    for dev in partners:
        pl.semaphore_signal(bar, inc=1, device_id=dev, device_id_type=MESH)
    pl.semaphore_wait(bar, len(partners))

    sends = []
    local1 = None
    for k, (dl, dy) in enumerate(ORDER):
        tl, ty = (zl + NL - dl) % NL, (y + NY - dy) % NY
        tg = tl * NY + ty
        for dc in range(NC):
            tc = (c + dc) % NC
            src = fac_hbm.at[0, pl.ds(2 * tg, 2), :, pl.ds(pl.multiple_of(tc * 256, 256), 256)]
            dst = b_v.at[k, :, zh, x, c]
            if dl == 0 and dy == 0 and dc == 0:
                local1 = pltpu.make_async_copy(src, dst, s1_r.at[k, dc])
                local1.start()
            else:
                cp = remote(src, dst, s1_s.at[k, dc], s1_r.at[k, dc], device(zh, x, tc, tl, ty))
                cp.start()
                sends.append(cp)

    def owner(k):
        dl, dy = ORDER[k]
        return ((zl + dl) % NL) * NY + (y + dy) % NY

    def gather(k):
        s = owner(k)

        def body(i, _):
            row = struct_ref[s, i]
            for j in range(2):
                col = struct_ref[s, 2 * grp + j] % 8
                a_v[k, j, c, i] = inv_v[row, col]
            return 0

        lax.fori_loop(0, 16, body, 0)
        cp = remote(a_v.at[k, :, c], a_v.at[k, :, c], a_s.at[k], a_r.at[k], device(zh, x, sib, zl, y))
        cp.start()
        sends.append(cp)

    def arrived(ref, sem):
        pltpu.make_async_copy(ref, ref, sem).wait()

    def stage_z(k):
        for dc in range(NC):
            src = (c + dc) % NC
            arrived(b_v.at[k, :, zh, x, src], s1_r.at[k, dc])
        for dz in range(1, NZ):
            blockref = b_v.at[k, :, zh, x]
            cp = remote(blockref, blockref, zs_s.at[k, dz - 1], zs_r.at[k, dz - 1],
                        device((zh + dz) % NZ, x, c, zl, y))
            cp.start()
            sends.append(cp)

    def stage_x(k):
        for dz in range(1, NZ):
            arrived(b_v.at[k, :, (zh + NZ - dz) % NZ, x], zs_r.at[k, dz - 1])
        blockref = b_v.at[k, :, :, x]
        for d, tx in enumerate((xr, xl)):
            cp = remote(blockref, blockref, x_s.at[k, d], x_r.at[k, d], device(zh, tx, c, zl, y))
            cp.start()
            sends.append(cp)

    def stage_w(k):
        for d, (fx, tx) in enumerate(((xl, xr), (xr, xl))):
            arrived(b_v.at[k, :, :, fx], x_r.at[k, d])
            blockref = b_v.at[k, d, :, fx]
            cp = remote(blockref, blockref, w_s.at[k, d], w_r.at[k, d], device(zh, tx, c, zl, y))
            cp.start()
            sends.append(cp)

    def compute(k):
        far = (x + 2) % NX
        for d in range(2):
            arrived(b_v.at[k, d, :, far], w_r.at[k, d])
        arrived(a_v.at[k, :, sib], a_r.at[k])
        dl, dy = ORDER[k]
        rhs = [b_v[k, j].reshape(512, 256) for j in range(2)]
        for r in range(NC):
            acc = jnp.dot(a_v[k, 0, r].reshape(256, 512), rhs[0], preferred_element_type=F32)
            acc += jnp.dot(a_v[k, 1, r].reshape(256, 512), rhs[1], preferred_element_type=F32)
            if dy == 0:
                c_own[pl.ds(256 * r, 256), :] = acc
            else:
                c_snd[k, pl.ds(256 * r, 256), :] = acc.astype(BF16)
        if dy:
            cp = remote(c_snd.at[k], c_rcv.at[dl, dy - 1], c_s.at[k], c_r.at[dl, dy - 1],
                        device(zh, x, c, zl, (y + dy) % NY))
            cp.start()
            sends.append(cp)

    def y_sum(dl, rows):
        total = c_own[rows, :]
        for n in range(NY - 1):
            total += c_rcv[dl, n, rows, :].astype(F32)
        return total

    def pass_on():
        for n in range(NY - 1):
            arrived(c_rcv.at[1, n], c_r.at[1, n])

        def body(n, _):
            rows = pl.ds(pl.multiple_of(n * 64, 64), 64)
            z_snd[rows, :] = y_sum(1, rows).astype(BF16)
            return 0

        lax.fori_loop(0, 8, body, 0)
        cp = remote(z_snd, z_rcv, q_s, q_r, device(zh, x, c, 1 - zl, y))
        cp.start()
        sends.append(cp)

    for t in range(steps + 3):
        if t < steps:
            stage_z(t)
        if 1 <= t <= steps:
            stage_x(t - 1)
        if t == 0:
            for cp in loads:
                cp.wait()
        if t < steps:
            gather(t)
        if t == 3:
            load_f.wait()
            cp = remote(f_v.at[c], f_v.at[c], fx_s, fx_r, device(zh, x, sib, zl, y))
            cp.start()
            sends.append(cp)
        if 2 <= t <= steps + 1:
            stage_w(t - 2)
        if t >= 3:
            if t - 3 == 5:
                pass_on()
            compute(t - 3)

    for n in range(NY - 1):
        arrived(c_rcv.at[0, n], c_r.at[0, n])
    arrived(z_rcv, q_r)

    def finish(n, _):
        rows = pl.ds(pl.multiple_of(n * 64, 64), 64)
        o_v[rows, :] = (-(y_sum(0, rows) + z_rcv[rows, :].astype(F32))).astype(BF16)
        return 0

    lax.fori_loop(0, 8, finish, 0)
    give = o_v.at[pl.ds(pl.multiple_of(sib * 256, 256), 256)]
    cp = remote(give, o_rcv, o_s, o_r, device(zh, x, sib, zl, y))
    cp.start()
    sends.append(cp)

    arrived(f_v.at[sib], fx_r)
    for n in range(2):
        cols = pl.ds(256 * n, 256)
        both = f_v[:, :, :, cols].reshape(512, 256)
        corr = lax.dot_general(both, o_v[...], (((0,), (0,)), ((), ())), preferred_element_type=F32)
        corr = corr.reshape(2, NX, 32, 256)
        g32[pl.ds(2 * n, 2)] = corr
        g_snd[pl.ds(2 * n, 2)] = corr.astype(BF16)
    for dx in range(1, NX):
        tx = (x + dx) % NX
        cp = remote(g_snd.at[:, tx], g_rcv.at[dx - 1], g_s.at[dx - 1], g_r.at[dx - 1],
                    device(zh, tx, c, zl, y))
        cp.start()
        sends.append(cp)
    for dx in range(1, NX):
        arrived(g_rcv.at[dx - 1], g_r.at[dx - 1])
    for n in range(NZ):
        total = g32[n, x]
        for dx in range(1, NX):
            total += g_rcv[dx - 1, n].astype(F32)
        h_snd[n] = total.astype(BF16).reshape(NC, 16, 256)
    for dz in range(NZ):
        tz = (zh + dz) % NZ
        for dc in range(NC):
            tc = (c + dc) % NC
            if dz == 0 and dc == 0:
                continue
            cp = remote(h_snd.at[tz, tc], h_rcv.at[dz, c], h_s.at[dz, dc], h_r.at[dz, dc],
                        device(tz, x, tc, zl, y))
            cp.start()
            sends.append(cp)
    h_rcv[0, c] = h_snd[zh, c]

    arrived(o_rcv, o_r)
    mine = pl.ds(pl.multiple_of(c * 256, 256), 256)
    other = pl.ds(pl.multiple_of(sib * 256, 256), 256)
    off_ref[0, :, :, mine] = o_v[mine, :].reshape(16, 16, 256)
    off_ref[0, :, :, other] = o_rcv[...].reshape(16, 16, 256)

    for dz in range(NZ):
        for dc in range(NC):
            if dz == 0 and dc == 0:
                continue
            arrived(h_rcv.at[dz, (c + dc) % NC], h_r.at[dz, dc])
    for half in range(NC):
        cols = slice(256 * half, 256 * half + 256)
        total = dif_ref[0, :, cols]
        for dz in range(NZ):
            total -= h_rcv[dz, half].astype(F32)
        diag_ref[0, :, cols] = total

    for cp in sends:
        cp.wait_send()


def on_device(inv_tiles, factor, diag_inv_factor, structure):
    vm = pltpu.VMEM
    dma = pltpu.SemaphoreType.DMA
    any_space = pl.BlockSpec(memory_space=pltpu.HBM)
    in_vmem = pl.BlockSpec(memory_space=pltpu.VMEM)
    return pl.pallas_call(
        kernel,
        out_shape=(
            jax.ShapeDtypeStruct((1, 16, 16, 512), BF16),
            jax.ShapeDtypeStruct((1, 16, 512), F32),
        ),
        in_specs=[pl.BlockSpec(memory_space=pltpu.SMEM), any_space, any_space, in_vmem],
        out_specs=(in_vmem, in_vmem),
        scratch_shapes=[
            vm((64, 8, 16, 512), BF16),
            vm((2, 16, 16, 512), BF16),
            vm((8, 2, 2, 16, 16, 512), BF16),
            vm((8, 2, NZ, NX, NC, 16, 256), BF16),
            vm((8, 512, 256), BF16),
            vm((2, NY - 1, 512, 256), BF16),
            vm((512, 256), F32),
            vm((512, 256), BF16),
            vm((512, 256), BF16),
            vm((512, 256), BF16),
            vm((256, 256), BF16),
            vm((NZ, NX, 32, 256), F32),
            vm((NZ, NX, 32, 256), BF16),
            vm((NX - 1, NZ, 32, 256), BF16),
            vm((NZ, NC, 16, 256), BF16),
            vm((NZ, NC, 16, 256), BF16),
            dma((8,)), dma(()),
            dma((8, 2)), dma((8, 2)),
            dma((8, 3)), dma((8, 3)),
            dma((8, 2)), dma((8, 2)),
            dma((8, 2)), dma((8, 2)),
            dma((8,)), dma((8,)),
            dma(()), dma(()),
            dma((8,)), dma((2, 3)),
            dma(()), dma(()),
            dma(()), dma(()),
            dma((3,)), dma((3,)),
            dma((4, 2)), dma((4, 2)),
        ],
        compiler_params=pltpu.CompilerParams(
            collective_id=0, has_side_effects=True, vmem_limit_bytes=48 << 20
        ),
    )(structure, inv_tiles, factor, diag_inv_factor)


def solution(mesh):
    return jax.shard_map(
        on_device,
        mesh=mesh,
        in_specs=(
            P(None, "grp", "blk", None),
            P("grp", None, "blk", None),
            P("grp", "blk", None),
            P(),
        ),
        out_specs=(P("grp", None, "blk", None), P("grp", "blk", None)),
        check_vma=False,
    )
```

time: 174 us -> 81.2 us (0.47)
  waiting for transfers between devices: 87.3 us -> 0 us
  Pallas kernels: 0 us -> 76.6 us
  blocking collectives: 45.7 us -> 0 us
  between operations: 14.1 us -> 0.65 us
  matrix products: 8.13 us -> 0 us
  starting transfers between devices: 8.12 us -> 0 us
  other arithmetic: 3.35 us -> 0 us
  local copies, waits for them, and re-layouts: 6.66 us -> 3.71 us
    pallas_call x0 -> x1, Pallas kernels: none -> 76.6 us  [on_device(): pl.pallas_call(kernel, out_shape=(jax.ShapeDtypeStruct((1, 16, 16, 512),...]
    all_gather x1 -> x0, waiting for transfers between devices: 69.7 us -> none  [on_device(): readers = lax.all_gather(received, 'blk', axis=2, tiled=True)]
    all_to_all x2 -> x0, blocking collectives: 45.7 us -> none  [the longest x1 33.1 us: sum_at_owner(): tiles = lax.all_to_all(split_up(shard, dim, count), axis, 0, 0, tiled=True)]
    all_to_all x1 -> x0, waiting for transfers between devices: 17.6 us -> none  [sum_at_owner(): tiles = lax.all_to_all(split_up(shard, dim, count), axis, 0, 0, tiled=True)]
    dot_general x2 -> x0, matrix products: 8.13 us -> none  [the longest x1 6.99 us: on_device(): jnp.einsum('crjxy,cjyz->crxz', selected, readers, preferred_element_type=...]
    all_to_all x1 -> x0, starting transfers between devices: 8.09 us -> none  [sum_at_owner(): tiles = lax.all_to_all(split_up(shard, dim, count), axis, 0, 0, tiled=True)]
    gather x1 -> x0, local copies, waits for them, and re-layouts: 6.51 us -> none  [on_device(): selected = inv_tiles[structure[:, :, None], local_cols[:, None, :]]]
    unnamed x4 -> x8, local copies, waits for them, and re-layouts: 0.01 us -> 3.71 us
  transfers between devices with their start and end apart: 2 -> 0, of which waited for: 2 -> 0; matrix products, arithmetic and copies ran while one was open for 5% -> 0% of each run, Pallas kernels for 0% -> 0%
where the time goes in v1:
time: 81.2 us; the launch traced here: 81 us
  Pallas kernels  76.6 us (94%)
  local copies, waits for them, and re-layouts  3.71 us (5%)
    pallas_call x1, Pallas kernels, on_device(): pl.pallas_call(kernel, out_shape=(jax.ShapeDtypeStruct((1, 16, 16, 512),...  76.6 us
    unnamed x8, local copies, waits for them, and re-layouts  3.71 us

profile of v1, /device:TPU:1, one launch (start us, length us, event | category | flops | bytes accessed | tf_op | source)
XLA Modules:
  0.0 81.0 jit_solution(16048285259077840392)
XLA Ops:
  0.6 0.0 copy-start
  0.6 0.9 %copy-done = bf16[1,16,16,512]{3,2,1,0:T(8,128)(2,1)S(1)} copy-done((bf16[1,16,16,512]{3,2,1,0:T(8,128)(2,1)S(1)}, bf16[1,16,16,512]{3,2,1,0:T(8,128)(2,1)}, u32[]{:S(2)}) %copy-start) | copy-done | bytes 262168
  1.6 0.0 copy-start.1
  1.6 0.8 copy-done.1
  2.3 0.0 copy-start.2
  2.3 0.7 copy-done.2
  3.0 76.6 %shard_map.59 = (bf16[1,16,16,512]{3,2,1,0:T(8,128)(2,1)S(1)}, f32[1,16,512]{2,1,0:T(8,128)S(1)}) custom-call(s32[8,16]{1,0:T(8,128)S(1)} %copy-done.2, bf16[64,8,16,512]{3,2,1,0:T(8,128)(2,1)} %inv_hbm.1, bf16[1,16,16,512]{3,2,1,0:T(8,128)(2,1)S(1)} %copy-done, f32[1,16,512]{2,1,0:T(8,128)S(1)} %copy-done.1), custom_call_target="tpu_custom_call" | custom-call | tf_op jit(solution)/shard_map/pallas_call | solution.py:274
  79.7 0.7 copy.8
  80.4 0.6 copy.9
Async XLA Ops:
  0.6 1.0 %copy-start = (bf16[1,16,16,512]{3,2,1,0:T(8,128)(2,1)S(1)}, bf16[1,16,16,512]{3,2,1,0:T(8,128)(2,1)}, u32[]{:S(2)}) copy-start(bf16[1,16,16,512]{3,2,1,0:T(8,128)(2,1)} %fac_hbm.1) | copy-start | bytes 786436
  1.6 0.8 copy-start.1
  2.3 0.7 copy-start.2

commit v2 on v0

v2 whole, which is shorter than its diff:
```python
import jax
import jax.numpy as jnp
from jax import lax
from jax.experimental import pallas as pl
from jax.experimental.pallas import tpu as pltpu
from jax.sharding import PartitionSpec as P

MESH = pl.DeviceIdType.MESH
BF16 = jnp.bfloat16
F32 = jnp.float32
NZ, NX, NC, NL, NY = 4, 4, 2, 2, 4
SLOTS = [(1, 0), (1, 2), (1, 1), (1, 3), (0, 2), (0, 1), (0, 3), (0, 0)]
OWN = 7
STEPS = [(k, 1, 0, 256) for k in range(5)] + [(5, 2, 0, 128), (5, 2, 128, 128), (OWN, 1, 0, 128), (OWN, 1, 128, 128)]
DIRECT = (8,)


def place():
    b = lax.axis_index("blk")
    g = lax.axis_index("grp")
    return b // (NX * NC), (b // NC) % NX, b % NC, g // NY, g % NY


def device(zh, x, c, zl, y):
    return {"blk": (zh * NX + x) * NC + c, "grp": zl * NY + y}


def kernel(
    struct_hbm, inv_hbm, fac_hbm, dif_hbm, off_ref, diag_ref,
    struct_s, inv_v, dif_v, f_v, ft_v, a_v, b_v, c_snd, c_rcv, c_own, z_snd, z_rcv,
    o_v, o_rcv, g32, g_snd, g_rcv, h_snd, h_rcv,
    ld_sem, s1_s, s1_r, zs_s, zs_r, x_s, x_r, w_s, w_r, a_s, a_r,
    fx_s, fx_r, c_s, c_r, q_s, q_r, o_s, o_r, g_s, g_r, h_s, h_r,
):
    zh, x, c, zl, y = place()
    sib = 1 - c
    grp = zl * NY + y
    xr, xl, far = (x + 1) % NX, (x + NX - 1) % NX, (x + 2) % NX
    sends = []
    clock = [0]

    def send(src, dst, ssem, rsem, dev):
        cp = pltpu.make_async_remote_copy(
            src_ref=src, dst_ref=dst, send_sem=ssem, recv_sem=rsem,
            device_id=dev, device_id_type=MESH)
        cp.start()
        sends.append((clock[0], cp))

    def settle(age):
        while sends and clock[0] - sends[0][0] >= age:
            sends.pop(0)[1].wait_send()

    def arrived(ref, sem):
        pltpu.make_async_copy(ref, ref, sem).wait()

    loads = [pltpu.make_async_copy(struct_hbm, struct_s, ld_sem.at[8])]
    for n in range(8):
        part = pl.ds(8 * n, 8)
        loads.append(pltpu.make_async_copy(inv_hbm.at[part], inv_v.at[part], ld_sem.at[n]))
    load_f = pltpu.make_async_copy(fac_hbm.at[0], f_v.at[c], ld_sem.at[9])
    load_d = pltpu.make_async_copy(dif_hbm, dif_v, ld_sem.at[10])

    offsets = [(0, 0, dc, dl, dy) for dl in range(NL) for dy in range(NY) for dc in range(NC)]
    offsets += [(dz, 0, dc, dl, dy) for dz in range(1, NZ) for dc in range(NC) for dl, dy in ((0, 0), SLOTS[0])]
    offsets += [(0, dx, 0, 0, 0) for dx in range(1, NX)]
    partners = [
        device((zh + dz) % NZ, (x + dx) % NX, (c + dc) % NC, (zl + dl) % NL, (y + dy) % NY)
        for dz, dx, dc, dl, dy in offsets if (dz, dx, dc, dl, dy) != (0, 0, 0, 0, 0)
    ]
    bar = pltpu.get_barrier_semaphore()
    for dev in partners:
        pl.semaphore_signal(bar, inc=1, device_id=dev, device_id_type=MESH)
    for cp in loads:
        cp.start()
    load_f.start()
    load_d.start()
    pl.semaphore_wait(bar, len(partners))

    def group_sends(slots, dzs):
        for k in slots:
            dl, dy = SLOTS[k]
            tl, ty = (zl + NL - dl) % NL, (y + NY - dy) % NY
            for dz in dzs:
                for dc in range(NC):
                    tc = (c + dc) % NC
                    src = fac_hbm.at[0, pl.ds(2 * (tl * NY + ty), 2), :, pl.ds(pl.multiple_of(tc * 256, 256), 256)]
                    dst = b_v.at[k, :, zh, x, c]
                    if (dl, dy, dz, dc) == (0, 0, 0, 0):
                        pltpu.make_async_copy(src, dst, s1_r.at[k, dz, dc]).start()
                    else:
                        send(src, dst, s1_s.at[k, dz, dc], s1_r.at[k, dz, dc],
                             device((zh + dz) % NZ, x, tc, tl, ty))

    def gather(k):
        dl, dy = SLOTS[k]
        s = ((zl + dl) % NL) * NY + (y + dy) % NY

        def body(i, _):
            row = struct_s[s, i]
            for j in range(2):
                a_v[k, j, c, i] = inv_v[row, struct_s[s, 2 * grp + j] % 8]
            return 0

        lax.fori_loop(0, 16, body, 0)
        send(a_v.at[k, :, c], a_v.at[k, :, c], a_s.at[k], a_r.at[k], device(zh, x, sib, zl, y))

    def stage_z(k):
        for dc in range(NC):
            arrived(b_v.at[k, :, zh, x, (c + dc) % NC], s1_r.at[k, 0, dc])
        ref = b_v.at[k, :, zh, x]
        for dz in range(1, NZ):
            send(ref, ref, zs_s.at[k, dz - 1], zs_r.at[k, dz - 1], device((zh + dz) % NZ, x, c, zl, y))

    def part(n, j, sz, sx):
        k, many, col, cols = STEPS[n]
        return b_v.at[pl.ds(k, many), j, sz, sx, :, :, pl.ds(col, cols)]

    every = slice(None)

    def stage_x(n):
        k, many, col, cols = STEPS[n]
        if n == 0:
            for dz in range(NZ):
                for dc in range(NC):
                    arrived(b_v.at[k, :, (zh + NZ - dz) % NZ, x, (c + dc) % NC], s1_r.at[k, dz, dc])
        elif col == 0:
            for m in range(k, k + many):
                for dz in range(1, NZ):
                    arrived(b_v.at[m, :, (zh + NZ - dz) % NZ, x], zs_r.at[m, dz - 1])
        ref = part(n, every, every, x)
        for d, tx in enumerate((xr, xl)):
            send(ref, ref, x_s.at[n, d], x_r.at[n, d], device(zh, tx, c, zl, y))
        if n in DIRECT:
            send(ref, ref, w_s.at[n, 0], w_r.at[n, 0], device(zh, far, c, zl, y))

    def stage_w(n):
        for d, (fx, tx) in enumerate(((xl, xr), (xr, xl))):
            arrived(part(n, every, every, fx), x_r.at[n, d])
            if n not in DIRECT:
                ref = part(n, d, every, fx)
                send(ref, ref, w_s.at[n, d], w_r.at[n, d], device(zh, tx, c, zl, y))

    def compute(n):
        k0, many, col, cols = STEPS[n]
        if n in DIRECT:
            arrived(part(n, every, every, far), w_r.at[n, 0])
        else:
            for d in range(2):
                arrived(part(n, d, every, far), w_r.at[n, d])
        lanes = slice(col, col + cols)
        for k in range(k0, k0 + many):
            dl, dy = SLOTS[k]
            if col == 0:
                arrived(a_v.at[k, :, sib], a_r.at[k])
            rhs = [b_v[k, j, :, :, :, :, lanes].reshape(512, cols) for j in range(2)]
            for r in range(NC):
                acc = jnp.dot(a_v[k, 0, r].reshape(256, 512), rhs[0], preferred_element_type=F32)
                acc += jnp.dot(a_v[k, 1, r].reshape(256, 512), rhs[1], preferred_element_type=F32)
                if dy == 0:
                    c_own[dl, pl.ds(256 * r, 256), lanes] = acc
                else:
                    c_snd[k, pl.ds(256 * r, 256), lanes] = acc.astype(BF16)
            if dy:
                half = col // 128
                send(c_snd.at[k, :, pl.ds(col, cols)], c_rcv.at[dl, dy - 1, :, pl.ds(col, cols)],
                     c_s.at[k, half], c_r.at[dl, dy - 1, half], device(zh, x, c, zl, (y + dy) % NY))

    def products(dl):
        for k0, many, col, cols in STEPS:
            for k in range(k0, k0 + many):
                if SLOTS[k][0] == dl and SLOTS[k][1]:
                    dy = SLOTS[k][1]
                    arrived(c_rcv.at[dl, dy - 1, :, pl.ds(col, cols)], c_r.at[dl, dy - 1, col // 128])

    def y_sum(dl, rows):
        total = c_own[dl, rows, :]
        for n in range(NY - 1):
            total += c_rcv[dl, n, rows, :].astype(F32)
        return total

    def pass_on():
        products(1)
        for n in range(8):
            rows = pl.ds(n * 64, 64)
            z_snd[rows, :] = y_sum(1, rows).astype(BF16)
        send(z_snd, z_rcv, q_s, q_r, device(zh, x, c, 1 - zl, y))

    def offdiag():
        products(0)
        arrived(z_rcv, q_r)
        for n in range(8):
            rows = pl.ds(n * 64, 64)
            o_v[rows, :] = (-(y_sum(0, rows) + z_rcv[rows, :].astype(F32))).astype(BF16)

    def correct():
        corr = jnp.dot(ft_v[...], o_v[...], preferred_element_type=F32).reshape(NZ, NX, 32, 256)
        g32[...] = corr
        g_snd[...] = corr.astype(BF16)
        for dx in (2, 1, 3):
            tx = (x + dx) % NX
            send(g_snd.at[:, tx], g_rcv.at[dx - 1], g_s.at[dx - 1], g_r.at[dx - 1], device(zh, tx, c, zl, y))
        give = o_v.at[pl.ds(pl.multiple_of(sib * 256, 256), 256)]
        send(give, o_rcv, o_s, o_r, device(zh, x, sib, zl, y))

    def x_sum():
        for dx in range(1, NX):
            arrived(g_rcv.at[dx - 1], g_r.at[dx - 1])
        for dz in (2, 1, 3, 0):
            tz = (zh + dz) % NZ
            total = g32[tz, x]
            for dx in range(1, NX):
                total += g_rcv[dx - 1, tz].astype(F32)
            h_snd[tz] = total.astype(BF16).reshape(NC, 16, 256)
            for dc in range(NC):
                tc = (c + dc) % NC
                if dz or dc:
                    send(h_snd.at[tz, tc], h_rcv.at[dz, c], h_s.at[dz, dc], h_r.at[dz, dc],
                         device(tz, x, tc, zl, y))
        h_rcv[0, c] = h_snd[zh, c]

    def write_off():
        arrived(o_rcv, o_r)
        mine = pl.ds(pl.multiple_of(c * 256, 256), 256)
        other = pl.ds(pl.multiple_of(sib * 256, 256), 256)
        off_ref[0, :, :, mine] = o_v[mine, :].reshape(16, 16, 256)
        off_ref[0, :, :, other] = o_rcv[...].reshape(16, 16, 256)

    def write_diag():
        for dz in range(NZ):
            for dc in range(NC):
                if dz or dc:
                    arrived(h_rcv.at[dz, (c + dc) % NC], h_r.at[dz, dc])
        for half in range(NC):
            cols = pl.ds(256 * half, 256)
            total = dif_v[0, :, cols]
            for dz in range(NZ):
                total -= h_rcv[dz, half].astype(F32)
            diag_ref[0, :, cols] = total

    def transpose_f():
        arrived(f_v.at[sib], fx_r)
        ft_v[...] = f_v[...].reshape(512, 512).T

    group_sends([0], range(NZ))
    group_sends(range(1, 8), [0])
    zs_at = {0: (1, 2), 1: (3,), 2: (4,), 3: (5, 6), 4: (7,)}
    steps = len(STEPS)
    for t in range(steps):
        clock[0] = t
        stage_x(t)
        for k in zs_at.get(t, ()):
            stage_z(k)
        if t == 0:
            for cp in loads:
                cp.wait()
        if t < 8:
            gather(t)
        if t >= 1:
            stage_w(t - 1)
        if t == 5:
            load_f.wait()
            send(f_v.at[c], f_v.at[c], fx_s, fx_r, device(zh, x, sib, zl, y))
        if t == 7:
            transpose_f()
            load_d.wait()
        if t == 7:
            pass_on()
        if t >= 2:
            compute(t - 2)
        settle(4)
    clock[0] = steps
    compute(steps - 2)
    stage_w(steps - 1)
    compute(steps - 1)
    offdiag()
    correct()
    settle(1)
    write_off()
    x_sum()
    write_diag()
    settle(0)


def on_device(inv_tiles, factor, diag_inv_factor, structure):
    vm = pltpu.VMEM
    dma = pltpu.SemaphoreType.DMA
    hbm = pl.BlockSpec(memory_space=pltpu.HBM)
    out = pl.BlockSpec(memory_space=pltpu.VMEM)
    return pl.pallas_call(
        kernel,
        out_shape=(
            jax.ShapeDtypeStruct((1, 16, 16, 512), BF16),
            jax.ShapeDtypeStruct((1, 16, 512), F32),
        ),
        in_specs=[hbm, hbm, hbm, hbm],
        out_specs=(out, out),
        scratch_shapes=[
            pltpu.SMEM((8, 16), jnp.int32),
            vm((64, 8, 16, 512), BF16),
            vm((1, 16, 512), F32),
            vm((2, 16, 16, 512), BF16),
            vm((512, 512), BF16),
            vm((8, 2, NC, 16, 16, 512), BF16),
            vm((8, 2, NZ, NX, NC, 16, 256), BF16),
            vm((7, 512, 256), BF16),
            vm((2, NY - 1, 512, 256), BF16),
            vm((2, 512, 256), F32),
            vm((512, 256), BF16),
            vm((512, 256), BF16),
            vm((512, 256), BF16),
            vm((256, 256), BF16),
            vm((NZ, NX, 32, 256), F32),
            vm((NZ, NX, 32, 256), BF16),
            vm((NX - 1, NZ, 32, 256), BF16),
            vm((NZ, NC, 16, 256), BF16),
            vm((NZ, NC, 16, 256), BF16),
            dma((11,)),
            dma((8, 4, 2)), dma((8, 4, 2)),
            dma((8, 3)), dma((8, 3)),
            dma((9, 2)), dma((9, 2)),
            dma((9, 2)), dma((9, 2)),
            dma((8,)), dma((8,)),
            dma(()), dma(()),
            dma((7, 2)), dma((2, 3, 2)),
            dma(()), dma(()),
            dma(()), dma(()),
            dma((3,)), dma((3,)),
            dma((4, 2)), dma((4, 2)),
        ],
        compiler_params=pltpu.CompilerParams(
            collective_id=0, has_side_effects=True, vmem_limit_bytes=48 << 20
        ),
    )(*[pltpu.with_memory_space_constraint(v, pltpu.HBM)
        for v in (structure, inv_tiles, factor, diag_inv_factor)])


def solution(mesh):
    return jax.shard_map(
        on_device,
        mesh=mesh,
        in_specs=(
            P(None, "grp", "blk", None),
            P("grp", None, "blk", None),
            P("grp", "blk", None),
            P(),
        ),
        out_specs=(P("grp", None, "blk", None), P("grp", "blk", None)),
        check_vma=False,
    )
```

time: 174 us -> 76.4 us (0.44)
  waiting for transfers between devices: 87.3 us -> 0 us
  Pallas kernels: 0 us -> 74.3 us
  blocking collectives: 45.7 us -> 0 us
  between operations: 14.1 us -> 0.64 us
  matrix products: 8.13 us -> 0 us
  starting transfers between devices: 8.12 us -> 0 us
  local copies, waits for them, and re-layouts: 6.66 us -> 1.32 us
  other arithmetic: 3.35 us -> 0 us
    pallas_call x0 -> x1, Pallas kernels: none -> 74.3 us  [on_device(): pl.pallas_call(kernel, out_shape=(jax.ShapeDtypeStruct((1, 16, 16, 512),...]
    all_gather x1 -> x0, waiting for transfers between devices: 69.7 us -> none  [on_device(): readers = lax.all_gather(received, 'blk', axis=2, tiled=True)]
    all_to_all x2 -> x0, blocking collectives: 45.7 us -> none  [the longest x1 33.1 us: sum_at_owner(): tiles = lax.all_to_all(split_up(shard, dim, count), axis, 0, 0, tiled=True)]
    all_to_all x1 -> x0, waiting for transfers between devices: 17.6 us -> none  [sum_at_owner(): tiles = lax.all_to_all(split_up(shard, dim, count), axis, 0, 0, tiled=True)]
    dot_general x2 -> x0, matrix products: 8.13 us -> none  [the longest x1 6.99 us: on_device(): jnp.einsum('crjxy,cjyz->crxz', selected, readers, preferred_element_type=...]
    all_to_all x1 -> x0, starting transfers between devices: 8.09 us -> none  [sum_at_owner(): tiles = lax.all_to_all(split_up(shard, dim, count), axis, 0, 0, tiled=True)]
    gather x1 -> x0, local copies, waits for them, and re-layouts: 6.51 us -> none  [on_device(): selected = inv_tiles[structure[:, :, None], local_cols[:, None, :]]]
  transfers between devices with their start and end apart: 2 -> 0, of which waited for: 2 -> 0; matrix products, arithmetic and copies ran while one was open for 5% -> 0% of each run, Pallas kernels for 0% -> 0%
where the time goes in v2:
time: 76.4 us; the launch traced here: 76.3 us
  Pallas kernels  74.3 us (97%)
  local copies, waits for them, and re-layouts  1.32 us (2%)
    pallas_call x1, Pallas kernels, on_device(): pl.pallas_call(kernel, out_shape=(jax.ShapeDtypeStruct((1, 16, 16, 512),...  74.3 us

profile of v2, /device:TPU:1, one launch (start us, length us, event | category | flops | bytes accessed | tf_op | source)
XLA Modules:
  0.0 76.3 jit_solution(2101029383342253964)
XLA Ops:
  0.6 74.3 %shard_map.59 = (bf16[1,16,16,512]{3,2,1,0:T(8,128)(2,1)S(1)}, f32[1,16,512]{2,1,0:T(8,128)S(1)}) custom-call(s32[8,16]{1,0:T(8,128)} %struct_hbm.1, bf16[64,8,16,512]{3,2,1,0:T(8,128)(2,1)} %inv_hbm.1, bf16[1,16,16,512]{3,2,1,0:T(8,128)(2,1)} %fac_hbm.1, f32[1,16,512]{2,1,0:T(8,128)} %dif_hbm.1), custom_call_target="tpu_custom_call" | custom-call | tf_op jit(solution)/shard_map/pallas_call | solution.py:289
  75.0 0.7 copy.8
  75.7 0.6 copy.9

commit v3 on v2

--- a/solution.py
+++ b/solution.py
@@ -28,9 +28,9 @@
 def kernel(
     struct_hbm, inv_hbm, fac_hbm, dif_hbm, off_ref, diag_ref,
     struct_s, inv_v, dif_v, f_v, ft_v, a_v, b_v, c_snd, c_rcv, c_own, z_snd, z_rcv,
-    o_v, o_rcv, g32, g_snd, g_rcv, h_snd, h_rcv,
+    o_v, o_rcv, g_snd, g_rcv,
     ld_sem, s1_s, s1_r, zs_s, zs_r, x_s, x_r, w_s, w_r, a_s, a_r,
-    fx_s, fx_r, c_s, c_r, q_s, q_r, o_s, o_r, g_s, g_r, h_s, h_r,
+    fx_s, fx_r, c_s, c_r, q_s, q_r, o_s, o_r, g_s, g_r,
 ):
     zh, x, c, zl, y = place()
     sib = 1 - c
@@ -193,30 +193,19 @@
             o_v[rows, :] = (-(y_sum(0, rows) + z_rcv[rows, :].astype(F32))).astype(BF16)
 
     def correct():
-        corr = jnp.dot(ft_v[...], o_v[...], preferred_element_type=F32).reshape(NZ, NX, 32, 256)
-        g32[...] = corr
-        g_snd[...] = corr.astype(BF16)
-        for dx in (2, 1, 3):
-            tx = (x + dx) % NX
-            send(g_snd.at[:, tx], g_rcv.at[dx - 1], g_s.at[dx - 1], g_r.at[dx - 1], device(zh, tx, c, zl, y))
+        corr = jnp.dot(ft_v[...], o_v[...], preferred_element_type=F32)
+        g_snd[...] = corr.astype(BF16).reshape(NZ, NX, NC, 16, 256)
+        for dz in (2, 1, 3, 0):
+            for dx in (2, 1, 3, 0):
+                for dc in range(NC):
+                    tz, tx, tc = (zh + dz) % NZ, (x + dx) % NX, (c + dc) % NC
+                    src, dst = g_snd.at[tz, tx, tc], g_rcv.at[dz, dx, c]
+                    if (dz, dx, dc) == (0, 0, 0):
+                        pltpu.make_async_copy(src, dst, g_r).start()
+                    else:
+                        send(src, dst, g_s.at[dz, dx, dc], g_r, device(tz, tx, tc, zl, y))
         give = o_v.at[pl.ds(pl.multiple_of(sib * 256, 256), 256)]
         send(give, o_rcv, o_s, o_r, device(zh, x, sib, zl, y))
-
-    def x_sum():
-        for dx in range(1, NX):
-            arrived(g_rcv.at[dx - 1], g_r.at[dx - 1])
-        for dz in (2, 1, 3, 0):
-            tz = (zh + dz) % NZ
-            total = g32[tz, x]
-            for dx in range(1, NX):
-                total += g_rcv[dx - 1, tz].astype(F32)
-            h_snd[tz] = total.astype(BF16).reshape(NC, 16, 256)
-            for dc in range(NC):
-                tc = (c + dc) % NC
-                if dz or dc:
-                    send(h_snd.at[tz, tc], h_rcv.at[dz, c], h_s.at[dz, dc], h_r.at[dz, dc],
-                         device(tz, x, tc, zl, y))
-        h_rcv[0, c] = h_snd[zh, c]
 
     def write_off():
         arrived(o_rcv, o_r)
@@ -226,15 +215,13 @@
         off_ref[0, :, :, other] = o_rcv[...].reshape(16, 16, 256)
 
     def write_diag():
-        for dz in range(NZ):
-            for dc in range(NC):
-                if dz or dc:
-                    arrived(h_rcv.at[dz, (c + dc) % NC], h_r.at[dz, dc])
+        arrived(g_rcv, g_r)
         for half in range(NC):
             cols = pl.ds(256 * half, 256)
             total = dif_v[0, :, cols]
             for dz in range(NZ):
-                total -= h_rcv[dz, half].astype(F32)
+                for dx in range(NX):
+                    total -= g_rcv[dz, dx, half].astype(F32)
             diag_ref[0, :, cols] = total
 
     def transpose_f():
@@ -276,7 +263,6 @@
     correct()
     settle(1)
     write_off()
-    x_sum()
     write_diag()
     settle(0)
 
@@ -309,11 +295,8 @@
             vm((512, 256), BF16),
             vm((512, 256), BF16),
             vm((256, 256), BF16),
-            vm((NZ, NX, 32, 256), F32),
-            vm((NZ, NX, 32, 256), BF16),
-            vm((NX - 1, NZ, 32, 256), BF16),
-            vm((NZ, NC, 16, 256), BF16),
-            vm((NZ, NC, 16, 256), BF16),
+            vm((NZ, NX, NC, 16, 256), BF16),
+            vm((NZ, NX, NC, 16, 256), BF16),
             dma((11,)),
             dma((8, 4, 2)), dma((8, 4, 2)),
             dma((8, 3)), dma((8, 3)),
@@ -324,8 +307,7 @@
             dma((7, 2)), dma((2, 3, 2)),
             dma(()), dma(()),
             dma(()), dma(()),
-            dma((3,)), dma((3,)),
-            dma((4, 2)), dma((4, 2)),
+            dma((NZ, NX, NC)), dma(()),
         ],
         compiler_params=pltpu.CompilerParams(
             collective_id=0, has_side_effects=True, vmem_limit_bytes=48 << 20

time: 76.4 us -> 74.7 us (0.978)
  Pallas kernels: 74.3 us -> 72.6 us
    pallas_call x1, Pallas kernels: 74.3 us -> 72.6 us  [on_device(): pl.pallas_call(kernel, out_shape=(jax.ShapeDtypeStruct((1, 16, 16, 512),...]
where the time goes in v3:
time: 74.7 us; the launch traced here: 74.6 us
  Pallas kernels  72.6 us (97%)
  local copies, waits for them, and re-layouts  1.32 us (2%)
    pallas_call x1, Pallas kernels, on_device(): pl.pallas_call(kernel, out_shape=(jax.ShapeDtypeStruct((1, 16, 16, 512),...  72.6 us

profile of v3, /device:TPU:1, one launch (start us, length us, event | category | flops | bytes accessed | tf_op | source)
XLA Modules:
  0.0 74.6 jit_solution(18254230977966961747)
XLA Ops:
  0.6 72.6 %shard_map.59 = (bf16[1,16,16,512]{3,2,1,0:T(8,128)(2,1)S(1)}, f32[1,16,512]{2,1,0:T(8,128)S(1)}) custom-call(s32[8,16]{1,0:T(8,128)} %struct_hbm.1, bf16[64,8,16,512]{3,2,1,0:T(8,128)(2,1)} %inv_hbm.1, bf16[1,16,16,512]{3,2,1,0:T(8,128)(2,1)} %fac_hbm.1, f32[1,16,512]{2,1,0:T(8,128)} %dif_hbm.1), custom_call_target="tpu_custom_call" | custom-call | tf_op jit(solution)/shard_map/pallas_call | solution.py:275
  73.3 0.7 copy.8
  74.0 0.6 copy.9

commit v4 on v3

--- a/solution.py
+++ b/solution.py
@@ -6,13 +6,19 @@
 from jax.sharding import PartitionSpec as P
 
 MESH = pl.DeviceIdType.MESH
+ZS = {0: (1,), 1: (2,), 2: (3,), 3: (4,), 4: (5,), 5: (6,), 6: (7,)}
+ZFIRST = False
+SLATE = ()
+GFIRST = True
+WLAG = 1
+CLAG = 2
 BF16 = jnp.bfloat16
 F32 = jnp.float32
 NZ, NX, NC, NL, NY = 4, 4, 2, 2, 4
 SLOTS = [(1, 0), (1, 2), (1, 1), (1, 3), (0, 2), (0, 1), (0, 3), (0, 0)]
 OWN = 7
-STEPS = [(k, 1, 0, 256) for k in range(5)] + [(5, 2, 0, 128), (5, 2, 128, 128), (OWN, 1, 0, 128), (OWN, 1, 128, 128)]
-DIRECT = (8,)
+STEPS = [(0, 1, 0, 128), (0, 1, 128, 128)] + [(k, 1, 0, 256) for k in range(1, 5)] + [(5, 2, 0, 128), (5, 2, 128, 128), (OWN, 1, 0, 128), (OWN, 1, 128, 128)]
+DIRECT = (9,)
 
 
 def place():
@@ -29,7 +35,7 @@
     struct_hbm, inv_hbm, fac_hbm, dif_hbm, off_ref, diag_ref,
     struct_s, inv_v, dif_v, f_v, ft_v, a_v, b_v, c_snd, c_rcv, c_own, z_snd, z_rcv,
     o_v, o_rcv, g_snd, g_rcv,
-    ld_sem, s1_s, s1_r, zs_s, zs_r, x_s, x_r, w_s, w_r, a_s, a_r,
+    ld_sem, m_s, m_r, s1_s, s1_r, zs_s, zs_r, x_s, x_r, w_s, w_r, a_s, a_r,
     fx_s, fx_r, c_s, c_r, q_s, q_r, o_s, o_r, g_s, g_r,
 ):
     zh, x, c, zl, y = place()
@@ -60,12 +66,12 @@
     load_f = pltpu.make_async_copy(fac_hbm.at[0], f_v.at[c], ld_sem.at[9])
     load_d = pltpu.make_async_copy(dif_hbm, dif_v, ld_sem.at[10])
 
-    offsets = [(0, 0, dc, dl, dy) for dl in range(NL) for dy in range(NY) for dc in range(NC)]
-    offsets += [(dz, 0, dc, dl, dy) for dz in range(1, NZ) for dc in range(NC) for dl, dy in ((0, 0), SLOTS[0])]
-    offsets += [(0, dx, 0, 0, 0) for dx in range(1, NX)]
+    offsets = [(0, 0, dc, dl, dy) for dl in range(NL) for dy in range(1, NY) for dc in range(NC)]
+    offsets += [(dz, 0, dc, 1, 0) for dz in range(NZ) for dc in range(NC)]
+    offsets += [(0, 1, 0, 0, 0), (0, NX - 1, 0, 0, 0)]
     partners = [
         device((zh + dz) % NZ, (x + dx) % NX, (c + dc) % NC, (zl + dl) % NL, (y + dy) % NY)
-        for dz, dx, dc, dl, dy in offsets if (dz, dx, dc, dl, dy) != (0, 0, 0, 0, 0)
+        for dz, dx, dc, dl, dy in offsets
     ]
     bar = pltpu.get_barrier_semaphore()
     for dev in partners:
@@ -91,6 +97,17 @@
                         send(src, dst, s1_s.at[k, dz, dc], s1_r.at[k, dz, dc],
                              device((zh + dz) % NZ, x, tc, tl, ty))
 
+    def merged_sends(half):
+        dl, dy = SLOTS[0]
+        tl, ty = (zl + NL - dl) % NL, (y + NY - dy) % NY
+        for dz in range(NZ):
+            for dc in range(NC):
+                tc = (c + dc) % NC
+                cols = pl.ds(pl.multiple_of(tc * 256 + 128 * half, 128), 128)
+                send(fac_hbm.at[0, pl.ds(2 * (tl * NY + ty), 2), :, cols],
+                     b_v.at[0, :, zh, x, c, :, pl.ds(128 * half, 128)],
+                     m_s.at[half, dz, dc], m_r.at[half, dz, dc], device((zh + dz) % NZ, x, tc, tl, ty))
+
     def gather(k):
         dl, dy = SLOTS[k]
         s = ((zl + dl) % NL) * NY + (y + dy) % NY
@@ -119,10 +136,11 @@
 
     def stage_x(n):
         k, many, col, cols = STEPS[n]
-        if n == 0:
+        if k == 0:
             for dz in range(NZ):
                 for dc in range(NC):
-                    arrived(b_v.at[k, :, (zh + NZ - dz) % NZ, x, (c + dc) % NC], s1_r.at[k, dz, dc])
+                    arrived(b_v.at[0, :, (zh + NZ - dz) % NZ, x, (c + dc) % NC, :, pl.ds(col, 128)],
+                            m_r.at[col // 128, dz, dc])
         elif col == 0:
             for m in range(k, k + many):
                 for dz in range(1, NZ):
@@ -228,37 +246,48 @@
         arrived(f_v.at[sib], fx_r)
         ft_v[...] = f_v[...].reshape(512, 512).T
 
-    group_sends([0], range(NZ))
-    group_sends(range(1, 8), [0])
-    zs_at = {0: (1, 2), 1: (3,), 2: (4,), 3: (5, 6), 4: (7,)}
+    merged_sends(0)
+    merged_sends(1)
+    group_sends([k for k in range(1, OWN) if k not in SLATE], [0])
     steps = len(STEPS)
+    done_w, done_c = 0, 0
     for t in range(steps):
         clock[0] = t
+        if ZFIRST:
+            for k in ZS.get(t, ()):
+                stage_z(k)
         stage_x(t)
-        for k in zs_at.get(t, ()):
-            stage_z(k)
+        if not ZFIRST:
+            for k in ZS.get(t, ()):
+                stage_z(k)
         if t == 0:
+            group_sends([*SLATE, OWN], [0])
             for cp in loads:
                 cp.wait()
-        if t < 8:
+        if GFIRST and t < 8:
             gather(t)
-        if t >= 1:
-            stage_w(t - 1)
+        if t >= WLAG:
+            stage_w(t - WLAG)
+        if not GFIRST and t < 8:
+            gather(t)
         if t == 5:
             load_f.wait()
             send(f_v.at[c], f_v.at[c], fx_s, fx_r, device(zh, x, sib, zl, y))
         if t == 7:
             transpose_f()
             load_d.wait()
-        if t == 7:
+        if t - CLAG == 6:
             pass_on()
-        if t >= 2:
-            compute(t - 2)
+        if t >= CLAG:
+            compute(t - CLAG)
         settle(4)
     clock[0] = steps
-    compute(steps - 2)
-    stage_w(steps - 1)
-    compute(steps - 1)
+    for n in range(steps - CLAG, steps):
+        if WLAG == 2 and n == steps - 3:
+            stage_w(steps - 2)
+        if n == steps - 1:
+            stage_w(steps - 1)
+        compute(n)
     offdiag()
     correct()
     settle(1)
@@ -298,10 +327,11 @@
             vm((NZ, NX, NC, 16, 256), BF16),
             vm((NZ, NX, NC, 16, 256), BF16),
             dma((11,)),
+            dma((2, 4, 2)), dma((2, 4, 2)),
             dma((8, 4, 2)), dma((8, 4, 2)),
             dma((8, 3)), dma((8, 3)),
-            dma((9, 2)), dma((9, 2)),
-            dma((9, 2)), dma((9, 2)),
+            dma((10, 2)), dma((10, 2)),
+            dma((10, 2)), dma((10, 2)),
             dma((8,)), dma((8,)),
             dma(()), dma(()),
             dma((7, 2)), dma((2, 3, 2)),

time: 74.7 us -> 74.2 us (level)
  no operation moved by 1% of the time
where the time goes in v4:
time: 74.2 us
  Pallas kernels  72.2 us (97%)
  local copies, waits for them, and re-layouts  1.32 us (2%)
    pallas_call x1, Pallas kernels, on_device(): pl.pallas_call(kernel, out_shape=(jax.ShapeDtypeStruct((1, 16, 16, 512),...  72.2 us

profile of v4, /device:TPU:1, one launch (start us, length us, event | category | flops | bytes accessed | tf_op | source)
XLA Modules:
  0.0 74.2 jit_solution(13397790549590008774)
XLA Ops:
  0.6 72.2 %shard_map.59 = (bf16[1,16,16,512]{3,2,1,0:T(8,128)(2,1)S(1)}, f32[1,16,512]{2,1,0:T(8,128)S(1)}) custom-call(s32[8,16]{1,0:T(8,128)} %struct_hbm.1, bf16[64,8,16,512]{3,2,1,0:T(8,128)(2,1)} %inv_hbm.1, bf16[1,16,16,512]{3,2,1,0:T(8,128)(2,1)} %fac_hbm.1, f32[1,16,512]{2,1,0:T(8,128)} %dif_hbm.1), custom_call_target="tpu_custom_call" | custom-call | tf_op jit(solution)/shard_map/pallas_call | solution.py:304
  72.8 0.7 copy.8
  73.5 0.6 copy.9
